TPU v7x, 512 devices: a whole 4x8x8 slice. The times are simulated.
512 devices in a mesh: sess: 16 (over z_hi, x), ctx: 32 (over y, z_lo, core).
Axes of the slice: x: 4, y: 8, z: 8 (z_hi: 4, z_lo: 2; z = z_hi * 2 + z_lo), core: 2. Of those that a mesh axis runs over, the one named last changes fastest.
Arguments:
- query_rows: bfloat16 [16, 2048, 4096], P('sess', 'ctx'), may hold values from -6 to 6
- key_rows: bfloat16 [16, 2048, 4096], P('sess', 'ctx'), may hold values from -6 to 6
- value_rows: bfloat16 [16, 2048, 4096], P('sess', 'ctx'), may hold values from -6 to 6
- seg_starts: int32 [16, 4], P('sess'), may hold values from 0 to 2047, as said below
- norm_gain: float32 [4096], replicated, may hold values from 0.1 to 1.9
Outputs:
- attended: bfloat16 [16, 2048, 4096], P('sess', 'ctx')
Inputs may be any that keep to these rules, and one draw needn't show every extreme that they name: `seg_starts`: within each session the starts rise strictly, the first is 0 and the last is 2047.
All inputs are finite; a program needn't handle non-finite values.
Results may differ from a plain program's by a relative error of at most 0.0049.
Values sent between devices are 32-bit elements; how exact they have to be, the bound alone decides.
A program may use at most 192 MiB of HBM per device.

v0:
```python
import jax
import jax.numpy as jnp
from jax import lax
from jax.sharding import PartitionSpec as P

HEADS = 32
HD = 128


def prefix(value, axis, join, neutral):
    count, mine = (lax.axis_size(axis), lax.axis_index(axis))
    pieces = jax.tree.map(lambda part: lax.all_gather(part, axis), value)
    total = jax.tree.map(
        lambda part, zero: jnp.full_like(part, 0) + jnp.asarray(zero, part.dtype), value, neutral
    )

    def step(position, total):
        longer = join(total, jax.tree.map(lambda part: part[position], pieces))
        return jax.tree.map(lambda new, old: jnp.where(position < mine, new, old), longer, total)

    return lax.fori_loop(0, count - 1, step, total)


def combine_states(earlier, later):
    flag_early, state_early = earlier
    flag_late, state_late = later
    return (jnp.maximum(flag_early, flag_late), state_late + (1.0 - flag_late[0]) * state_early)


def shards(query_rows, key_rows, value_rows, seg_starts, norm_gain):
    rows = query_rows.shape[1]
    width = query_rows.shape[2]
    block_start = lax.axis_index("ctx") * rows
    positions = block_start + jnp.arange(rows, dtype=jnp.int32)
    start_list = seg_starts[0]
    seg_ids = jnp.sum((start_list[None, :] <= positions[:, None]).astype(jnp.int32), axis=1)
    prior_count = jnp.sum((start_list < block_start).astype(jnp.int32))
    query_heads = query_rows[0].reshape(rows, HEADS, HD)
    key_heads = key_rows[0].reshape(rows, HEADS, HD)
    value_heads = value_rows[0].reshape(rows, HEADS, HD)
    last_seg = seg_ids[-1]
    keep_mask = (seg_ids == last_seg).astype(jnp.bfloat16)
    kept_keys = key_heads * keep_mask[:, None, None]
    reset_flag = (last_seg != prior_count).astype(jnp.float32).reshape(1)
    summary = jnp.einsum("uhe,uhf->hef", kept_keys, value_heads, preferred_element_type=jnp.float32)
    identity = (jnp.zeros((1,), jnp.float32), jnp.zeros_like(summary))
    flags_in, state_in = prefix((reset_flag, summary), "ctx", combine_states, identity)
    causal = jnp.arange(rows)[:, None] >= jnp.arange(rows)[None, :]
    allowed = causal & (seg_ids[:, None] == seg_ids[None, :])
    scores = jnp.einsum("the,uhe->htu", query_heads, key_heads, preferred_element_type=jnp.float32)
    weights = jnp.where(allowed[None], scores, 0.0).astype(jnp.bfloat16)
    intra = jnp.einsum("htu,uhe->the", weights, value_heads, preferred_element_type=jnp.float32)
    carried = state_in.astype(jnp.bfloat16)
    inter = jnp.einsum("the,hef->thf", query_heads, carried, preferred_element_type=jnp.float32)
    use_mask = (seg_ids == prior_count).astype(jnp.float32)
    mixed = (intra + use_mask[:, None, None] * inter).reshape(rows, width)
    scale_inv = lax.rsqrt(jnp.mean(mixed * mixed, axis=-1, keepdims=True) + 1e-05)
    attended = (mixed * scale_inv * norm_gain).astype(jnp.bfloat16)
    return attended.reshape(1, rows, width)


def solution(mesh):
    placed = (
        P("sess", "ctx", None),
        P("sess", "ctx", None),
        P("sess", "ctx", None),
        P("sess", None),
        P(),
    )
    return jax.shard_map(
        shards, mesh=mesh, in_specs=placed, out_specs=P("sess", "ctx", None), check_vma=False
    )
```

profile of v0, /device:TPU:1, one launch (start us, length us, event | category | flops | bytes accessed | tf_op | source)
XLA Modules:
  0.0 533.8 jit_solution(17027958208056277047)
XLA Ops:
  19.2 60.5 %all-reduce = f32[32]{0:T(128)S(1)} all-reduce(f32[32]{0:T(128)S(1)} %dynamic-update-slice), channel_id=1, replica_groups=mesh['sess'=16,'ctx'=32] {'ctx'}, use_global_device_ids=true, to_apply=%add | all-reduce | flops 32 | bytes 256
  82.5 295.4 %all-gather.3.cloned.1.call-done = f32[1024,128,128]{2,1,0:T(8,128)} async-done(((f32[32,128,128]{2,1,0:T(8,128)}), f32[1024,128,128]{2,1,0:T(8,128)}) %all-gather.3.cloned.1.call-update) | async-done | bytes 67108880 | tf_op jit(solution)/shard_map/all_gather | solution.py:12
  377.9 145.4 %while.14 = (s32[]{:T(128)}, f32[32,128,128]{2,1,0:T(8,128)S(1)}, s32[]{:T(128)}, f32[32,32,128,128]{3,2,1,0:T(8,128)}, f32[32,1]{0,1:T(1,128)S(1)}, /*index=5*/s32[]{:T(128)}, s32[]{:T(128)}) while((s32[]{:T(128)}, f32[32,128,128]{2,1,0:T(8,128)S(1)}, s32[]{:T(128)}, f32[32,32,128,128]{3,2,1,0:T(8,128)}, f32[32,1]{0,1:T(1,128)S(1)}, ...), condition=%wide.region_3.4_spmd.clone, body=%wide.region_2.3_spmd.clone.sunk | while | flops 2097157 | bytes 6291573 | solution.py:21
  378.4 4.1 fusion.25
  383.1 4.1 fusion.25
  387.8 4.1 fusion.25
  392.5 4.1 fusion.25
  397.2 4.1 fusion.25
  401.9 4.1 fusion.25
  406.6 4.1 fusion.25
  411.3 4.1 fusion.25
  416.0 4.1 fusion.25
  420.7 4.1 fusion.25
  425.4 4.1 fusion.25
  430.0 4.1 fusion.25
  434.7 4.1 fusion.25
  439.4 4.1 fusion.25
  444.1 4.1 fusion.25
  448.8 4.1 fusion.25
  453.5 4.1 fusion.25
  458.2 4.1 fusion.25
  462.9 4.1 fusion.25
  467.6 4.1 fusion.25
  472.3 4.1 fusion.25
  477.0 4.1 fusion.25
  481.7 4.1 fusion.25
  486.4 4.1 fusion.25
  491.0 4.1 fusion.25
  495.7 4.1 fusion.25
  500.4 4.1 fusion.25
  505.1 4.1 fusion.25
  509.8 4.1 fusion.25
  (59 shorter events, 44.1 us)
Async XLA Ops:
  6.5 371.3 %all-gather.3.cloned.1.call-start = ((), (), s32[]{:S(2)}) async-start(), calls=%async_computation | async-start | bytes 69206016 | tf_op jit(solution)/shard_map/all_gather | solution.py:12
  11.5 1.3 copy-start
  525.1 0.8 copy-start.1
Sparse Core Ops, SparseCore 0:
  14.9 362.9 all-gather.2
where the time goes:
time: 535 us; the launch traced here: 534 us
  waiting for transfers between devices  295 us (55%)
  other arithmetic  149 us (28%)
  blocking collectives  60.5 us (11%)
  between operations  14.8 us (3%)
  local copies, waits for them, and re-layouts  6.84 us (1%)
  matrix products  6.5 us (1%)
    all_gather x1, waiting for transfers between devices, prefix(): pieces = jax.tree.map(lambda part: lax.all_gather(part, axis), value)  295 us
    select_n x31, other arithmetic, step(): jnp.where(position < mine, new, old)  127 us
    unnamed x1, blocking collectives  60.5 us
    sub x31, other arithmetic, combine_states(): 1.0 - flag_late[0]  18.2 us
  transfers between devices with their start and end apart: 1, of which 1 were waited for; matrix products, arithmetic and copies ran while one was open for 1% of the time, Pallas kernels for 0%

commit v1 on v0

v1 whole, which is shorter than its diff:
```python
import functools

import jax
import jax.numpy as jnp
from jax import lax
from jax.experimental import pallas as pl
from jax.experimental.pallas import tpu as pltpu
from jax.sharding import PartitionSpec as P

HEADS = 32
HD = 128
OWN = 8
SUB = 2
ROWS = HD // SUB
CHUNKS = OWN * SUB
RING = 8
MESH = pl.DeviceIdType.MESH
F32 = jnp.float32


def rows_at(i):
    return pl.ds(pl.multiple_of(i * ROWS, ROWS), ROWS)


def kernel(starts, q_ref, k_ref, v_ref, gain_ref, out_ref,
           own, kept, core_in, chip_far, chip_own, chip_in, scan_out, scan_in,
           back_out, back_in, core_out, carry_in, carry, mixed,
           sa, ra, sb, rb, sd, rd, se, re, sf, rf):
    me = lax.axis_index("ctx")
    core = me % 2
    half = (me // 2) % 2
    ring = me // 4
    tok = q_ref.shape[0]
    base = me * tok

    twin = {"ctx": me + 1 - 2 * core}
    across = {"ctx": me + 2 - 4 * half}
    ahead = {"ctx": (me + 4) % (4 * RING)}
    behind = {"ctx": (me + 4 * RING - 4) % (4 * RING)}

    barrier = pltpu.get_barrier_semaphore()
    for other in (twin, across, ahead, behind):
        pl.semaphore_signal(barrier, inc=1, device_id=other, device_id_type=MESH)

    start = [starts[0, n] for n in range(4)]

    def keep(low, size):
        inside = [jnp.where((s >= low) & (s < low + size), 1, 0) for s in start]
        return jnp.where(sum(inside) == 0, 1.0, 0.0).astype(F32)

    chip_base = (me // 2) * (2 * tok)
    ring_base = ring * (4 * tok)
    keep_core0 = keep(chip_base, tok)
    keep_core1 = keep(chip_base + tok, tok)
    keep_chip0 = keep(ring_base, 2 * tok)
    keep_chip1 = keep(ring_base + 2 * tok, 2 * tok)
    keep_ring = keep(ring_base, 4 * tok)
    one, nil = jnp.float32(1.0), jnp.float32(0.0)
    first_core, first_half = core == 0, half == 0
    a_own = jnp.where(first_core, keep_core1, one)
    a_in = jnp.where(first_core, one, keep_core1)
    b_own = jnp.where(first_half, keep_chip1, one)
    b_in = jnp.where(first_half, one, keep_chip1)
    e_own, e_scan = jnp.where(first_half, one, nil), jnp.where(first_half, keep_chip0, one)
    p_in, p_scan = jnp.where(first_half, nil, one), jnp.where(first_half, one, keep_chip0)
    f_own, f_pre = jnp.where(first_core, one, nil), jnp.where(first_core, keep_core0, one)
    g_in, g_pre = jnp.where(first_core, nil, one), jnp.where(first_core, one, keep_core0)

    def segment(pos):
        return sum((s <= pos).astype(jnp.int32) for s in start)

    row = lax.broadcasted_iota(jnp.int32, (tok, 1), 0) + base
    col = lax.broadcasted_iota(jnp.int32, (1, tok), 1) + base
    seg_row, seg_col = segment(row), segment(col)
    prior = sum(jnp.where(s < base, 1, 0) for s in start)
    last = sum(jnp.where(s < base + tok, 1, 0) for s in start)
    use = jnp.where(seg_row == prior, 1.0, 0.0).astype(F32)
    allowed = (row >= col) & (seg_row == seg_col)
    keep_rows = jnp.where(seg_row == last, 1.0, 0.0).astype(k_ref.dtype)

    def head_cols(h):
        return pl.ds(pl.multiple_of(h * HD, HD), HD)

    def group(c, z):
        return (2 * c + z) * OWN

    kept[...] = k_ref[...] * keep_rows

    def send_core(z, j):
        return pltpu.make_async_remote_copy(
            src_ref=own.at[group(1 - core, z) + j], dst_ref=core_in.at[z * OWN + j],
            send_sem=sa.at[z * OWN + j], recv_sem=ra.at[z * OWN + j],
            device_id=twin, device_id_type=MESH)

    def send_chip(i):
        return pltpu.make_async_remote_copy(
            src_ref=chip_far.at[rows_at(i)], dst_ref=chip_in.at[rows_at(i)],
            send_sem=sb.at[i], recv_sem=rb.at[i], device_id=across, device_id_type=MESH)

    def send_scan(i):
        return pltpu.make_async_remote_copy(
            src_ref=scan_out.at[rows_at(i)], dst_ref=scan_in.at[rows_at(i)],
            send_sem=sd.at[i], recv_sem=rd.at[i], device_id=ahead, device_id_type=MESH)

    def send_back(i):
        return pltpu.make_async_remote_copy(
            src_ref=back_out.at[rows_at(i)], dst_ref=back_in.at[rows_at(i)],
            send_sem=se.at[i], recv_sem=re.at[i], device_id=across, device_id_type=MESH)

    def send_carry(z, i):
        n = z * CHUNKS + i
        return pltpu.make_async_remote_copy(
            src_ref=core_out.at[rows_at(n)], dst_ref=carry_in.at[rows_at(n)],
            send_sem=sf.at[n], recv_sem=rf.at[n], device_id=twin, device_id_type=MESH)

    def summary(h):
        own[h] = lax.dot_general(
            kept[:, head_cols(h)], v_ref[:, head_cols(h)], (((0,), (0,)), ((), ())),
            preferred_element_type=F32)

    for j in range(OWN):
        summary(group(1 - core, 1 - half) + j)
    pl.semaphore_wait(barrier, 4)
    for j in range(OWN):
        send_core(1 - half, j).start()
    for j in range(OWN):
        summary(group(core, 1 - half) + j)
        summary(group(1 - core, half) + j)
        send_core(half, j).start()

    def far(j, _):
        n = (1 - half) * OWN + j
        send_core(1 - half, j).wait_recv()
        total = a_own * own[group(core, 1 - half) + j] + a_in * core_in[n]
        chip_far[pl.ds(pl.multiple_of(j * HD, HD), HD)] = total
        for s in range(SUB):
            send_chip(j * SUB + s).start()
        return 0

    lax.fori_loop(0, OWN, far, 0)
    for j in range(OWN):
        summary(group(core, half) + j)

    def near(j, _):
        n = half * OWN + j
        send_core(half, j).wait_recv()
        chip_own[pl.ds(pl.multiple_of(j * HD, HD), HD)] = (
            a_own * own[group(core, half) + j] + a_in * core_in[n])
        return 0

    lax.fori_loop(0, OWN, near, 0)

    @pl.when(ring == 0)
    def _():
        scan_in[...] = jnp.zeros_like(scan_in)

    def spread(z, i, prefix):
        h, sub = group(core, z) + i // SUB, pl.ds(pl.multiple_of((i % SUB) * ROWS, ROWS), ROWS)
        n = z * CHUNKS + i
        core_out[rows_at(n)] = f_own * own[h, sub] + f_pre * prefix
        send_carry(z, i).start()
        carry[rows_at(n)] = (g_in * core_in[z * OWN + i // SUB, sub] + g_pre * prefix).astype(carry.dtype)

    def intra(h):
        cols = head_cols(h)
        scores = lax.dot_general(
            q_ref[:, cols], k_ref[:, cols], (((1,), (1,)), ((), ())), preferred_element_type=F32)
        weights = jnp.where(allowed, scores, 0.0).astype(v_ref.dtype)
        mixed[:, cols] = jnp.dot(weights, v_ref[:, cols], preferred_element_type=F32)

    def scan(i, _):
        send_chip(i).wait_recv()
        arrived, mine = chip_in[rows_at(i)], chip_own[rows_at(i)]

        @pl.when(ring > 0)
        def _():
            send_scan(i).wait_recv()

        prefix = scan_in[rows_at(i)]

        @pl.when(ring < RING - 1)
        def _():
            scan_out[rows_at(i)] = b_own * mine + b_in * arrived + keep_ring * prefix
            send_scan(i).start()

        back_out[rows_at(i)] = e_own * mine + e_scan * prefix
        send_back(i).start()
        spread(half, i, p_in * arrived + p_scan * prefix)
        for n in range(HEADS // CHUNKS):
            intra(i * (HEADS // CHUNKS) + n)
        return 0

    lax.fori_loop(0, CHUNKS, scan, 0)

    def back(i, _):
        send_back(i).wait_recv()
        spread(1 - half, i, back_in[rows_at(i)])
        return 0

    lax.fori_loop(0, CHUNKS, back, 0)

    def join(h, state, squares):
        cols = head_cols(h)
        inter = jnp.dot(q_ref[:, cols], state, preferred_element_type=F32)
        value = mixed[:, cols] + use * inter
        mixed[:, cols] = value
        return squares + value * value

    def join_own(n, squares):
        return join(group(core, 0) + n, carry[pl.ds(pl.multiple_of(n * HD, HD), HD)], squares)

    def join_in(n, squares):
        for s in range(SUB):
            send_carry(n // OWN, (n % OWN) * SUB + s).wait_recv()
        state = carry_in[pl.ds(pl.multiple_of(n * HD, HD), HD)].astype(carry.dtype)
        return join(group(1 - core, 0) + n, state, squares)

    squares = lax.fori_loop(0, 2 * OWN, join_own, jnp.zeros((tok, HD), F32))
    squares = lax.fori_loop(0, 2 * OWN, join_in, squares)
    mean = jnp.sum(squares, axis=-1, keepdims=True) * (1.0 / (HEADS * HD))
    scale = lax.rsqrt(mean + 1e-05)
    for h in range(HEADS):
        cols = slice(h * HD, (h + 1) * HD)
        out_ref[:, cols] = (mixed[:, cols] * scale * gain_ref[:, cols]).astype(out_ref.dtype)

    def drain(i, _):
        send_chip(i).wait_send()
        send_back(i).wait_send()
        send_carry(0, i).wait_send()
        send_carry(1, i).wait_send()

        @pl.when(ring < RING - 1)
        def _():
            send_scan(i).wait_send()

        return 0

    def drain_core(j, _):
        send_core(0, j).wait_send()
        send_core(1, j).wait_send()
        return 0

    lax.fori_loop(0, OWN, drain_core, 0)
    lax.fori_loop(0, CHUNKS, drain, 0)


def shards(query_rows, key_rows, value_rows, seg_starts, norm_gain):
    _, tok, width = query_rows.shape
    dma = pltpu.SemaphoreType.DMA
    vmem = pl.BlockSpec(memory_space=pltpu.VMEM)
    out = pl.pallas_call(
        kernel,
        out_shape=jax.ShapeDtypeStruct((tok, width), query_rows.dtype),
        in_specs=[pl.BlockSpec(memory_space=pltpu.SMEM), vmem, vmem, vmem, vmem],
        out_specs=vmem,
        scratch_shapes=[
            pltpu.VMEM((HEADS, HD, HD), F32),
            pltpu.VMEM((tok, width), key_rows.dtype),
            pltpu.VMEM((2 * OWN, HD, HD), F32),
            pltpu.VMEM((OWN * HD, HD), F32),
            pltpu.VMEM((OWN * HD, HD), F32),
            pltpu.VMEM((OWN * HD, HD), F32),
            pltpu.VMEM((OWN * HD, HD), F32),
            pltpu.VMEM((OWN * HD, HD), F32),
            pltpu.VMEM((OWN * HD, HD), F32),
            pltpu.VMEM((OWN * HD, HD), F32),
            pltpu.VMEM((2 * OWN * HD, HD), F32),
            pltpu.VMEM((2 * OWN * HD, HD), F32),
            pltpu.VMEM((2 * OWN * HD, HD), jnp.bfloat16),
            pltpu.VMEM((tok, width), F32),
            dma((2 * OWN,)), dma((2 * OWN,)),
            dma((CHUNKS,)), dma((CHUNKS,)),
            dma((CHUNKS,)), dma((CHUNKS,)),
            dma((CHUNKS,)), dma((CHUNKS,)),
            dma((2 * CHUNKS,)), dma((2 * CHUNKS,)),
        ],
        compiler_params=pltpu.CompilerParams(collective_id=0, has_side_effects=True),
    )(seg_starts, query_rows[0], key_rows[0], value_rows[0], norm_gain.reshape(1, width))
    return out.reshape(1, tok, width)


def solution(mesh):
    placed = (
        P("sess", "ctx", None),
        P("sess", "ctx", None),
        P("sess", "ctx", None),
        P("sess", None),
        P(),
    )
    return jax.shard_map(
        shards, mesh=mesh, in_specs=placed, out_specs=P("sess", "ctx", None), check_vma=False
    )
```

time: 535 us -> 54.8 us (0.10)
  the two profiles are of different devices: /device:TPU:1 before, /device:TPU:56 now
where the time goes in v1:
time: 54.8 us; the launch traced here: 54.7 us
  Pallas kernels  52.8 us (96%)
  local copies, waits for them, and re-layouts  1.87 us (3%)
    pallas_call x1, Pallas kernels, shards(): pl.pallas_call(kernel, out_shape=jax.ShapeDtypeStruct((tok, width), query...  52.8 us
    unnamed x1, local copies, waits for them, and re-layouts  1.87 us

profile of v1, /device:TPU:56, one launch (start us, length us, event | category | flops | bytes accessed | tf_op | source)
XLA Modules:
  0.0 54.7 jit_solution(14176770093441037892)
XLA Ops:
  0.0 52.8 %shard_map.55 = bf16[64,4096]{1,0:T(8,128)(2,1)} custom-call(s32[1,4]{1,0:T(1,128)} %starts.1, bf16[64,4096]{1,0:T(8,128)(2,1)} %bitcast.6, bf16[64,4096]{1,0:T(8,128)(2,1)} %bitcast.7, bf16[64,4096]{1,0:T(8,128)(2,1)} %bitcast.8, f32[1,4096]{1,0:T(1,128)} %bitcast.9), custom_call_target="tpu_custom_call" | custom-call | tf_op jit(solution)/shard_map/pallas_call | solution.py:251
  52.8 1.9 %copy.7 = bf16[1,64,4096]{2,1,0:T(8,128)(2,1)} copy(bf16[1,64,4096]{2,1,0:T(8,128)(2,1)} %bitcast.5) | data formatting | bytes 1048576

commit v2 on v1

v2 whole, which is shorter than its diff:
```python
import jax
import jax.numpy as jnp
from jax import lax
from jax.experimental import pallas as pl
from jax.experimental.pallas import tpu as pltpu
from jax.sharding import PartitionSpec as P

HEADS = 32
HD = 128
OWN = 8
SUB = 4
ROWS = HD // SUB
CHUNKS = OWN * SUB
RING = 8
MID = RING // 2
HOP = 8
BACK = 9
DRAINED = 38
MESH = pl.DeviceIdType.MESH
F32 = jnp.float32


def rows_at(i):
    return pl.ds(pl.multiple_of(i * ROWS, ROWS), ROWS)


def head_rows(n):
    return pl.ds(pl.multiple_of(n * HD, HD), HD)


def head_cols(h):
    return pl.ds(pl.multiple_of(h * HD, HD), HD)


def kernel(starts_hbm, q_hbm, k_hbm, v_hbm, gain_hbm, out_ref,
           starts, q_ref, k_ref, v_ref, gain_ref,
           own, kept, core_in, chip_far, chip_own, chip_in, total,
           fore_out, fore_in, local_out, local_in, rear_out, rear_in,
           back_out, back_in, core_out, carry_in, carry, mixed,
           loads, core_sent, core_got, chip_sent, chip_got, fore_sent, fore_got,
           local_sent, local_got, rear_sent, rear_got, back_sent, back_got, carry_sent, carry_got):
    me = lax.axis_index("ctx")
    core = me % 2
    half = (me // 2) % 2
    ring = me // 4
    tok = q_ref.shape[0]
    base = me * tok

    twin = {"ctx": me + 1 - 2 * core}
    across = {"ctx": me + 2 - 4 * half}
    ahead = {"ctx": (me + 4) % (4 * RING)}
    behind = {"ctx": (me + 4 * RING - 4) % (4 * RING)}

    barrier = pltpu.get_barrier_semaphore()
    for other in (twin, across, ahead, behind):
        pl.semaphore_signal(barrier, inc=1, device_id=other, device_id_type=MESH)

    fetches = [
        pltpu.make_async_copy(src, dst, loads.at[n])
        for n, (src, dst) in enumerate((
            (starts_hbm, starts), (k_hbm, k_ref), (v_hbm, v_ref), (q_hbm, q_ref), (gain_hbm, gain_ref)))]
    for fetch in fetches:
        fetch.start()
    fetches[0].wait()

    start = [starts[0, n] for n in range(4)]

    def keep(low, size):
        inside = [jnp.where((s >= low) & (s < low + size), 1, 0) for s in start]
        return jnp.where(sum(inside) == 0, 1.0, 0.0).astype(F32)

    chip_base = (me // 2) * (2 * tok)
    span = 4 * tok
    ring_base = ring * span
    keep_core0 = keep(chip_base, tok)
    keep_core1 = keep(chip_base + tok, tok)
    keep_chip0 = keep(ring_base, 2 * tok)
    keep_chip1 = keep(ring_base + 2 * tok, 2 * tok)
    keep_ring = keep(ring_base, span)
    keep_local = keep(MID * span, ring_base - MID * span)
    one, nil = jnp.float32(1.0), jnp.float32(0.0)
    keep_rear = jnp.where(ring >= MID, nil, keep(ring_base + span, (MID - 1 - ring) * span))
    first_core, first_half = core == 0, half == 0
    a_own = jnp.where(first_core, keep_core1, one)
    a_in = jnp.where(first_core, one, keep_core1)
    b_own = jnp.where(first_half, keep_chip1, one)
    b_in = jnp.where(first_half, one, keep_chip1)
    e_own, e_scan = jnp.where(first_half, one, nil), jnp.where(first_half, keep_chip0, one)
    p_in, p_scan = jnp.where(first_half, nil, one), jnp.where(first_half, one, keep_chip0)
    f_own, f_pre = jnp.where(first_core, one, nil), jnp.where(first_core, keep_core0, one)
    g_in, g_pre = jnp.where(first_core, nil, one), jnp.where(first_core, one, keep_core0)

    def segment(pos):
        return sum((s <= pos).astype(jnp.int32) for s in start)

    row = lax.broadcasted_iota(jnp.int32, (tok, 1), 0) + base
    col = lax.broadcasted_iota(jnp.int32, (1, tok), 1) + base
    seg_row, seg_col = segment(row), segment(col)
    prior = sum(jnp.where(s < base, 1, 0) for s in start)
    last = sum(jnp.where(s < base + tok, 1, 0) for s in start)
    use = jnp.where(seg_row == prior, 1.0, 0.0).astype(F32)
    allowed = (row >= col) & (seg_row == seg_col)
    keep_rows = jnp.where(seg_row == last, 1.0, 0.0).astype(k_ref.dtype)

    def group(c, z):
        return (2 * c + z) * OWN

    def remote(src, dst, sent, got, device):
        return pltpu.make_async_remote_copy(
            src_ref=src, dst_ref=dst, send_sem=sent, recv_sem=got,
            device_id=device, device_id_type=MESH)

    def send_core(z, j):
        return remote(own.at[head_rows(group(1 - core, z) + j)], core_in.at[head_rows(z * OWN + j)],
                      core_sent, core_got.at[z * OWN + j], twin)

    def send_chip(i):
        return remote(chip_far.at[rows_at(i)], chip_in.at[rows_at(i)],
                      chip_sent, chip_got.at[i], across)

    def send_fore(i):
        return remote(fore_out.at[rows_at(i)], fore_in.at[rows_at(i)],
                      fore_sent, fore_got.at[i], ahead)

    def send_local(i):
        return remote(local_out.at[rows_at(i)], local_in.at[rows_at(i)],
                      local_sent, local_got.at[i], ahead)

    def send_rear(i):
        return remote(rear_out.at[rows_at(i)], rear_in.at[rows_at(i)],
                      rear_sent, rear_got.at[i], behind)

    def send_back(i):
        return remote(back_out.at[rows_at(i)], back_in.at[rows_at(i)],
                      back_sent, back_got.at[i], across)

    def send_carry(n):
        return remote(core_out.at[rows_at(n)], carry_in.at[rows_at(n)],
                      carry_sent, carry_got.at[n], twin)

    def summaries(first):
        states = [lax.dot_general(
            kept[:, head_cols(first + j)], v_ref[:, head_cols(first + j)],
            (((0,), (0,)), ((), ())), preferred_element_type=F32) for j in range(OWN)]
        for j in range(OWN):
            own[head_rows(first + j)] = states[j]

    fetches[1].wait()
    kept[...] = k_ref[...] * keep_rows
    fetches[2].wait()
    summaries(group(1 - core, 1 - half))
    summaries(group(core, 1 - half))
    pl.semaphore_wait(barrier, 4)
    for j in range(OWN):
        send_core(1 - half, j).start()
    summaries(group(1 - core, half))
    for j in range(OWN):
        send_core(half, j).start()
    summaries(group(core, half))

    def chip_total(z, j):
        send_core(z, j).wait_recv()
        return a_own * own[head_rows(group(core, z) + j)] + a_in * core_in[head_rows(z * OWN + j)]

    def far(j, _):
        chip_far[head_rows(j)] = chip_total(1 - half, j)
        for s in range(SUB):
            send_chip(j * SUB + s).start()
        return 0

    def near(j, _):
        chip_own[head_rows(j)] = chip_total(half, j)
        return 0

    lax.fori_loop(0, OWN, far, 0)
    lax.fori_loop(0, OWN, near, 0)

    @pl.when(ring == 0)
    def _():
        fore_in[...] = jnp.zeros_like(fore_in)

    @pl.when(ring == MID)
    def _():
        local_in[...] = jnp.zeros_like(local_in)

    @pl.when(ring == MID - 1)
    def _():
        rear_in[...] = jnp.zeros_like(rear_in)

    def intra(n, _):
        cols = [head_cols(n * 8 + m) for m in range(8)]
        scores = [lax.dot_general(
            q_ref[:, c], k_ref[:, c], (((1,), (1,)), ((), ())), preferred_element_type=F32)
            for c in cols]
        weights = [jnp.where(allowed, s, 0.0).astype(v_ref.dtype) for s in scores]
        values = [jnp.dot(w, v_ref[:, c], preferred_element_type=F32) for w, c in zip(weights, cols)]
        for c, value in zip(cols, values):
            mixed[:, c] = value
        return 0

    fetches[3].wait()
    fetches[4].wait()
    early = ring >= MID

    @pl.when(early)
    def _():
        lax.fori_loop(0, HEADS // 8, intra, 0)

    def spread(z, i, prefix):
        n = z * CHUNKS + i
        core_out[rows_at(n)] = f_own * own[rows_at(group(core, z) * SUB + i)] + f_pre * prefix
        send_carry(n).start()
        carry[rows_at(n)] = (g_in * core_in[rows_at(n)] + g_pre * prefix).astype(carry.dtype)

    def finish(i, prefix):
        arrived, mine = chip_in[rows_at(i)], chip_own[rows_at(i)]
        back_out[rows_at(i)] = e_own * mine + e_scan * prefix
        send_back(i).start()
        spread(half, i, p_in * arrived + p_scan * prefix)

    last_fore = MID + 1
    lag_local = HOP * (ring - MID)
    lag_fore = HOP * ring
    lag_rear = HOP * ((RING + MID - 1 - ring) % RING)
    lag_back = jnp.maximum(jnp.where(ring <= last_fore, lag_fore, lag_rear) + BACK, DRAINED)

    def active(s, lag):
        return (s >= lag) & (s < lag + CHUNKS)

    def step(s, _):
        @pl.when(s < CHUNKS)
        def _():
            send_chip(s).wait_recv()
            total[rows_at(s)] = b_own * chip_own[rows_at(s)] + b_in * chip_in[rows_at(s)]

        @pl.when((ring >= MID) & active(s, lag_local))
        def _():
            i = s - lag_local

            @pl.when(ring > MID)
            def _():
                send_local(i).wait_recv()

            @pl.when(ring < RING - 1)
            def _():
                local_out[rows_at(i)] = total[rows_at(i)] + keep_ring * local_in[rows_at(i)]
                send_local(i).start()

        @pl.when((ring <= last_fore) & active(s, lag_fore))
        def _():
            i = s - lag_fore

            @pl.when(ring > 0)
            def _():
                send_fore(i).wait_recv()

            prefix = fore_in[rows_at(i)]

            @pl.when(ring < last_fore)
            def _():
                fore_out[rows_at(i)] = total[rows_at(i)] + keep_ring * prefix
                send_fore(i).start()

            finish(i, prefix)

        @pl.when(((ring < MID) | (ring > last_fore)) & active(s, lag_rear))
        def _():
            i = s - lag_rear

            @pl.when(ring != MID - 1)
            def _():
                send_rear(i).wait_recv()

            @pl.when((ring < MID) | (ring == RING - 1))
            def _():
                rear_out[rows_at(i)] = rear_in[rows_at(i)] + keep_rear * total[rows_at(i)]
                send_rear(i).start()

            @pl.when(ring > last_fore)
            def _():
                finish(i, local_in[rows_at(i)] + keep_local * rear_in[rows_at(i)])

        @pl.when(active(s, lag_back))
        def _():
            i = s - lag_back
            send_back(i).wait_recv()
            spread(1 - half, i, back_in[rows_at(i)])

        return 0

    lax.fori_loop(0, lag_back + CHUNKS, step, 0)

    @pl.when(jnp.logical_not(early))
    def _():
        lax.fori_loop(0, HEADS // 8, intra, 0)

    def settle(j, squares):
        heads, states = [], []
        for z in (half, 1 - half):
            heads.append(group(core, z) + j)
            states.append(carry[head_rows(z * OWN + j)])
        for z in (half, 1 - half):
            for s in range(SUB):
                send_carry(z * CHUNKS + j * SUB + s).wait_recv()
            heads.append(group(1 - core, z) + j)
            states.append(carry_in[head_rows(z * OWN + j)].astype(carry.dtype))
        cols = [head_cols(h) for h in heads]
        inter = [jnp.dot(q_ref[:, c], state, preferred_element_type=F32) for c, state in zip(cols, states)]
        values = [mixed[:, c] + use * part for c, part in zip(cols, inter)]
        for c, value in zip(cols, values):
            mixed[:, c] = value
        return squares + sum(value * value for value in values)

    squares = lax.fori_loop(0, OWN, settle, jnp.zeros((tok, HD), F32))
    mean = jnp.sum(squares, axis=-1, keepdims=True) * (1.0 / (HEADS * HD))
    scale = lax.rsqrt(mean + 1e-05)
    for h in range(HEADS):
        cols = slice(h * HD, (h + 1) * HD)
        out_ref[:, cols] = (mixed[:, cols] * scale * gain_ref[:, cols]).astype(out_ref.dtype)

    for z in range(2):
        part = pl.ds(pl.multiple_of(group(1 - core, z) * HD, HD), OWN * HD)
        remote(own.at[part], core_in.at[pl.ds(z * OWN * HD, OWN * HD)], core_sent, core_got.at[0], twin).wait_send()
    remote(chip_far, chip_in, chip_sent, chip_got.at[0], across).wait_send()
    remote(back_out, back_in, back_sent, back_got.at[0], across).wait_send()
    remote(core_out, carry_in, carry_sent, carry_got.at[0], twin).wait_send()

    @pl.when(ring < last_fore)
    def _():
        remote(fore_out, fore_in, fore_sent, fore_got.at[0], ahead).wait_send()

    @pl.when((ring >= MID) & (ring < RING - 1))
    def _():
        remote(local_out, local_in, local_sent, local_got.at[0], ahead).wait_send()

    @pl.when((ring < MID) | (ring == RING - 1))
    def _():
        remote(rear_out, rear_in, rear_sent, rear_got.at[0], behind).wait_send()


def shards(query_rows, key_rows, value_rows, seg_starts, norm_gain):
    _, tok, width = query_rows.shape
    dma = pltpu.SemaphoreType.DMA
    hbm = pl.BlockSpec(memory_space=pltpu.HBM)
    block = pltpu.VMEM((tok, width), key_rows.dtype)
    states = lambda heads: pltpu.VMEM((heads * HD, HD), F32)
    one = dma(())
    stay = lambda x: pltpu.with_memory_space_constraint(x, pltpu.HBM)
    out = pl.pallas_call(
        kernel,
        out_shape=jax.ShapeDtypeStruct((tok, width), query_rows.dtype),
        in_specs=[hbm] * 5,
        out_specs=pl.BlockSpec(memory_space=pltpu.VMEM),
        scratch_shapes=[
            pltpu.SMEM((1, 4), jnp.int32), block, block, block, pltpu.VMEM((1, width), F32),
            states(HEADS), block, states(2 * OWN),
            states(OWN), states(OWN), states(OWN), states(OWN),
            states(OWN), states(OWN), states(OWN), states(OWN), states(OWN), states(OWN),
            states(OWN), states(OWN), states(2 * OWN), states(2 * OWN),
            pltpu.VMEM((2 * OWN * HD, HD), jnp.bfloat16),
            pltpu.VMEM((tok, width), F32),
            dma((5,)),
            one, dma((2 * OWN,)), one, dma((CHUNKS,)), one, dma((CHUNKS,)),
            one, dma((CHUNKS,)), one, dma((CHUNKS,)), one, dma((CHUNKS,)), one, dma((2 * CHUNKS,)),
        ],
        compiler_params=pltpu.CompilerParams(
            collective_id=0, has_side_effects=True, vmem_limit_bytes=32 * 1024 * 1024),
    )(stay(seg_starts), stay(query_rows[0]), stay(key_rows[0]), stay(value_rows[0]),
      stay(norm_gain.reshape(1, width)))
    return out.reshape(1, tok, width)


def solution(mesh):
    placed = (
        P("sess", "ctx", None),
        P("sess", "ctx", None),
        P("sess", "ctx", None),
        P("sess", None),
        P(),
    )
    return jax.shard_map(
        shards, mesh=mesh, in_specs=placed, out_specs=P("sess", "ctx", None), check_vma=False
    )
```

time: 54.8 us -> 42.1 us (0.77)
  the two profiles are of different devices: /device:TPU:56 before, /device:TPU:48 now
where the time goes in v2:
time: 42.1 us; the launch traced here: 41.9 us
  Pallas kernels  41.1 us (98%)
  local copies, waits for them, and re-layouts  0.8 us (2%)
    pallas_call x1, Pallas kernels, shards(): pl.pallas_call(kernel, out_shape=jax.ShapeDtypeStruct((tok, width), query...  41.1 us

profile of v2, /device:TPU:48, one launch (start us, length us, event | category | flops | bytes accessed | tf_op | source)
XLA Modules:
  0.0 41.9 jit_solution(6832052982402696501)
XLA Ops:
  0.0 41.1 %shard_map.55 = bf16[64,4096]{1,0:T(8,128)(2,1)S(1)} custom-call(s32[1,4]{1,0:T(1,128)} %starts_hbm.1, bf16[64,4096]{1,0:T(8,128)(2,1)} %bitcast.6, bf16[64,4096]{1,0:T(8,128)(2,1)} %bitcast.7, bf16[64,4096]{1,0:T(8,128)(2,1)} %bitcast.8, f32[1,4096]{1,0:T(1,128)} %bitcast.9), custom_call_target="tpu_custom_call" | custom-call | tf_op jit(solution)/shard_map/pallas_call | solution.py:349
  41.1 0.8 %copy.7 = bf16[1,64,4096]{2,1,0:T(8,128)(2,1)} copy(bf16[1,64,4096]{2,1,0:T(8,128)(2,1)S(1)} %bitcast.5) | data formatting | bytes 1048576

commit v3 on v2

v3 whole, which is shorter than its diff:
```python
import jax
import jax.numpy as jnp
from jax import lax
from jax.experimental import pallas as pl
from jax.experimental.pallas import tpu as pltpu
from jax.sharding import PartitionSpec as P

HEADS = 32
HD = 128
OWN = 8
SUB = 4
ROWS = HD // SUB
CHUNKS = OWN * SUB
RING = 8
MID = RING // 2
HOP = 8
BACK = 9
JOIN = 8
DRAINED = 44
MESH = pl.DeviceIdType.MESH
F32 = jnp.float32


def rows_at(i):
    return pl.ds(pl.multiple_of(i * ROWS, ROWS), ROWS)


def head_rows(n):
    return pl.ds(pl.multiple_of(n * HD, HD), HD)


def head_cols(h):
    return pl.ds(pl.multiple_of(h * HD, HD), HD)


def kernel(starts_hbm, q_hbm, k_hbm, v_hbm, gain_hbm, out_ref,
           starts, q_ref, k_ref, v_ref, gain_ref,
           own, core_in, chip_far, chip_own, chip_in, total,
           fore_out, fore_in, local_out, local_in, rear_out, rear_in,
           back_out, back_in, core_out, carry_in, carry, mixed, squares,
           loads, core_sent, core_got, chip_sent, chip_got, fore_sent, ring_got,
           local_sent, rear_sent, back_sent, back_got, carry_sent, carry_got):
    me = lax.axis_index("ctx")
    core = me % 2
    half = (me // 2) % 2
    ring = me // 4
    tok = q_ref.shape[0]
    base = me * tok

    twin = {"ctx": me + 1 - 2 * core}
    across = {"ctx": me + 2 - 4 * half}
    ahead = {"ctx": (me + 4) % (4 * RING)}
    behind = {"ctx": (me + 4 * RING - 4) % (4 * RING)}

    last_fore = MID + 1

    def group(c, z):
        return (2 * c + z) * OWN

    def group_rows(c, z):
        return pl.ds(pl.multiple_of(group(c, z) * HD, HD), OWN * HD)

    order = [(1 - core, 1 - half), (core, 1 - half), (1 - core, half), (core, half)]
    fetch_starts = pltpu.make_async_copy(starts_hbm, starts, loads.at[0])
    fetch_keys = [pltpu.make_async_copy(
        k_hbm.at[:, group_rows(*g)], k_ref.at[:, group_rows(*g)], loads.at[1 + n]) for n, g in enumerate(order)]
    fetch_values = [pltpu.make_async_copy(
        v_hbm.at[:, group_rows(*g)], v_ref.at[:, group_rows(*g)], loads.at[5 + n]) for n, g in enumerate(order)]
    fetch_rest = [pltpu.make_async_copy(q_hbm, q_ref, loads.at[9]),
                  pltpu.make_async_copy(gain_hbm, gain_ref, loads.at[10])]
    fetch_starts.start()
    fetch_keys[0].start()
    fetch_values[0].start()
    barrier = pltpu.get_barrier_semaphore()
    for other in (twin, across, ahead, behind):
        pl.semaphore_signal(barrier, inc=1, device_id=other, device_id_type=MESH)

    for n in range(1, 4):
        fetch_keys[n].start()
        fetch_values[n].start()
    for fetch in fetch_rest:
        fetch.start()
    fetch_starts.wait()

    start = [starts[0, n] for n in range(4)]

    def keep(low, size):
        inside = [jnp.where((s >= low) & (s < low + size), 1, 0) for s in start]
        return jnp.where(sum(inside) == 0, 1.0, 0.0).astype(F32)

    chip_base = (me // 2) * (2 * tok)
    span = 4 * tok
    ring_base = ring * span
    keep_core0 = keep(chip_base, tok)
    keep_core1 = keep(chip_base + tok, tok)
    keep_chip0 = keep(ring_base, 2 * tok)
    keep_chip1 = keep(ring_base + 2 * tok, 2 * tok)
    keep_ring = keep(ring_base, span)
    keep_local = keep(MID * span, ring_base - MID * span)
    one, nil = jnp.float32(1.0), jnp.float32(0.0)
    keep_rear = jnp.where(ring >= MID, nil, keep(ring_base + span, (MID - 1 - ring) * span))
    first_core, first_half = core == 0, half == 0
    a_own = jnp.where(first_core, keep_core1, one)
    a_in = jnp.where(first_core, one, keep_core1)
    b_own = jnp.where(first_half, keep_chip1, one)
    b_in = jnp.where(first_half, one, keep_chip1)
    e_own, e_scan = jnp.where(first_half, one, nil), jnp.where(first_half, keep_chip0, one)
    p_in, p_scan = jnp.where(first_half, nil, one), jnp.where(first_half, one, keep_chip0)
    f_own, f_pre = jnp.where(first_core, one, nil), jnp.where(first_core, keep_core0, one)
    g_in, g_pre = jnp.where(first_core, nil, one), jnp.where(first_core, one, keep_core0)

    def segment(pos):
        return sum((s <= pos).astype(jnp.int32) for s in start)

    row = lax.broadcasted_iota(jnp.int32, (tok, 1), 0) + base
    col = lax.broadcasted_iota(jnp.int32, (1, tok), 1) + base
    seg_row, seg_col = segment(row), segment(col)
    prior = sum(jnp.where(s < base, 1, 0) for s in start)
    last = sum(jnp.where(s < base + tok, 1, 0) for s in start)
    use = jnp.where(seg_row == prior, 1.0, 0.0).astype(F32)
    allowed = (row >= col) & (seg_row == seg_col)
    keep_rows = jnp.where(seg_row == last, 1.0, 0.0).astype(k_ref.dtype)

    def remote(src, dst, sent, got, device):
        return pltpu.make_async_remote_copy(
            src_ref=src, dst_ref=dst, send_sem=sent, recv_sem=got,
            device_id=device, device_id_type=MESH)

    def send_core(j):
        z = 1 - half
        return remote(own.at[head_rows(group(1 - core, z) + j)], core_in.at[head_rows(z * OWN + j)],
                      core_sent, core_got.at[j], twin)

    def send_rest():
        return remote(own.at[group_rows(1 - core, half)], core_in.at[pl.ds(half * OWN * HD, OWN * HD)],
                      core_sent, core_got.at[OWN], twin)

    def send_chip(i):
        return remote(chip_far.at[rows_at(i)], chip_in.at[rows_at(i)],
                      chip_sent, chip_got.at[i], across)

    def send_fore(i):
        return remote(fore_out.at[rows_at(i)], fore_in.at[rows_at(i)],
                      fore_sent, ring_got.at[i], ahead)

    def local_lane(place):
        return jnp.where(place == last_fore, CHUNKS, 0)

    def send_local(i, place):
        return remote(local_out.at[rows_at(i)], local_in.at[rows_at(i)],
                      local_sent, ring_got.at[local_lane(place) + i], ahead)

    def send_rear(i):
        return remote(rear_out.at[rows_at(i)], rear_in.at[rows_at(i)],
                      rear_sent, ring_got.at[CHUNKS + i], behind)

    def send_back(i):
        return remote(back_out.at[rows_at(i)], back_in.at[rows_at(i)],
                      back_sent, back_got.at[i], across)

    def send_carry(n):
        return remote(core_out.at[head_rows(n)], carry_in.at[head_rows(n)],
                      carry_sent, carry_got.at[n], twin)

    def summaries(n):
        fetch_keys[n].wait()
        fetch_values[n].wait()
        first = group(*order[n])
        states = []
        for j in range(OWN):
            cols = head_cols(first + j)
            states.append(lax.dot_general(
                k_ref[:, cols] * keep_rows, v_ref[:, cols],
                (((0,), (0,)), ((), ())), preferred_element_type=F32))
        for j in range(OWN):
            own[head_rows(first + j)] = states[j]

    summaries(0)
    pl.semaphore_wait(barrier, 4)
    for j in range(OWN):
        send_core(j).start()
    summaries(1)

    def chip_total(z, j):
        return a_own * own[head_rows(group(core, z) + j)] + a_in * core_in[head_rows(z * OWN + j)]

    def far(j, _):
        send_core(j).wait_recv()
        chip_far[head_rows(j)] = chip_total(1 - half, j)
        for s in range(SUB):
            send_chip(j * SUB + s).start()
        return 0

    def near(j, _):
        chip_own[head_rows(j)] = chip_total(half, j)
        return 0

    lax.fori_loop(0, OWN, far, 0)
    summaries(2)
    send_rest().start()
    summaries(3)

    @pl.when(ring == 0)
    def _():
        fore_in[...] = jnp.zeros_like(fore_in)

    @pl.when(ring == MID)
    def _():
        local_in[...] = jnp.zeros_like(local_in)

    @pl.when(ring == MID - 1)
    def _():
        rear_in[...] = jnp.zeros_like(rear_in)

    def intra(n, _):
        cols = [head_cols(n * 8 + m) for m in range(8)]
        scores = [lax.dot_general(
            q_ref[:, c], k_ref[:, c], (((1,), (1,)), ((), ())), preferred_element_type=F32)
            for c in cols]
        weights = [jnp.where(allowed, s, 0.0).astype(v_ref.dtype) for s in scores]
        values = [jnp.dot(w, v_ref[:, c], preferred_element_type=F32) for w, c in zip(weights, cols)]
        for c, value in zip(cols, values):
            mixed[:, c] = value
        return 0

    for fetch in fetch_rest:
        fetch.wait()
    squares[...] = jnp.zeros_like(squares)
    lax.fori_loop(0, HEADS // 8, intra, 0)
    send_rest().wait_recv()
    lax.fori_loop(0, OWN, near, 0)

    def spread(z, i, prefix):
        n = z * CHUNKS + i
        core_out[rows_at(n)] = f_own * own[rows_at(group(core, z) * SUB + i)] + f_pre * prefix
        carry[rows_at(n)] = (g_in * core_in[rows_at(n)] + g_pre * prefix).astype(carry.dtype)

        @pl.when(i % SUB == SUB - 1)
        def _():
            send_carry(z * OWN + i // SUB).start()

    def finish(i, prefix):
        arrived, mine = chip_in[rows_at(i)], chip_own[rows_at(i)]
        back_out[rows_at(i)] = e_own * mine + e_scan * prefix
        send_back(i).start()
        spread(half, i, p_in * arrived + p_scan * prefix)

    lag_local = HOP * (ring - MID)
    lag_fore = HOP * ring
    lag_rear = HOP * ((RING + MID - 1 - ring) % RING)
    ends = (ring > MID) & (ring < RING - 1)
    lag_prefix = jnp.where(ring <= last_fore, lag_fore, lag_rear)
    lag_back = jnp.where(ends, lag_prefix + BACK, jnp.maximum(lag_prefix + 2 * BACK, DRAINED))
    lag_join = lag_back + SUB + JOIN

    def settle(j):
        heads, states = [], []
        for z in (half, 1 - half):
            heads.append(group(core, z) + j)
            states.append(carry[head_rows(z * OWN + j)])
        for z in (half, 1 - half):
            send_carry(z * OWN + j).wait_recv()
            heads.append(group(1 - core, z) + j)
            states.append(carry_in[head_rows(z * OWN + j)].astype(carry.dtype))
        cols = [head_cols(h) for h in heads]
        inter = [jnp.dot(q_ref[:, c], state, preferred_element_type=F32) for c, state in zip(cols, states)]
        values = [mixed[:, c] + use * part for c, part in zip(cols, inter)]
        for c, value in zip(cols, values):
            mixed[:, c] = value
        squares[...] += sum(value * value for value in values)

    def active(s, lag):
        return (s >= lag) & (s < lag + CHUNKS)

    def step(s, _):
        @pl.when(s < CHUNKS)
        def _():
            send_chip(s).wait_recv()
            total[rows_at(s)] = b_own * chip_own[rows_at(s)] + b_in * chip_in[rows_at(s)]

        @pl.when((ring >= MID) & active(s, lag_local))
        def _():
            i = s - lag_local

            @pl.when(ring > MID)
            def _():
                send_local(i, ring).wait_recv()

            @pl.when(ring < RING - 1)
            def _():
                local_out[rows_at(i)] = total[rows_at(i)] + keep_ring * local_in[rows_at(i)]
                send_local(i, ring + 1).start()

        @pl.when((ring <= last_fore) & active(s, lag_fore))
        def _():
            i = s - lag_fore

            @pl.when(ring > 0)
            def _():
                send_fore(i).wait_recv()

            prefix = fore_in[rows_at(i)]

            @pl.when(ring < last_fore)
            def _():
                fore_out[rows_at(i)] = total[rows_at(i)] + keep_ring * prefix
                send_fore(i).start()

            finish(i, prefix)

        @pl.when(((ring < MID) | (ring > last_fore)) & active(s, lag_rear))
        def _():
            i = s - lag_rear

            @pl.when(ring != MID - 1)
            def _():
                send_rear(i).wait_recv()

            @pl.when((ring < MID) | (ring == RING - 1))
            def _():
                rear_out[rows_at(i)] = rear_in[rows_at(i)] + keep_rear * total[rows_at(i)]
                send_rear(i).start()

            @pl.when(ring > last_fore)
            def _():
                finish(i, local_in[rows_at(i)] + keep_local * rear_in[rows_at(i)])

        @pl.when(active(s, lag_back))
        def _():
            i = s - lag_back
            send_back(i).wait_recv()
            spread(1 - half, i, back_in[rows_at(i)])

        @pl.when((s >= lag_join) & ((s - lag_join) % SUB == 0))
        def _():
            settle((s - lag_join) // SUB)

        return 0

    lax.fori_loop(0, lag_join + CHUNKS - SUB + 1, step, 0)

    mean = jnp.sum(squares[...], axis=-1, keepdims=True) * (1.0 / (HEADS * HD))
    scale = lax.rsqrt(mean + 1e-05)
    for h in range(HEADS):
        cols = slice(h * HD, (h + 1) * HD)
        out_ref[:, cols] = (mixed[:, cols] * scale * gain_ref[:, cols]).astype(out_ref.dtype)

    for z in range(2):
        remote(own.at[group_rows(1 - core, z)], core_in.at[pl.ds(z * OWN * HD, OWN * HD)],
               core_sent, core_got.at[0], twin).wait_send()
    remote(chip_far, chip_in, chip_sent, chip_got.at[0], across).wait_send()
    remote(back_out, back_in, back_sent, back_got.at[0], across).wait_send()
    remote(core_out, carry_in, carry_sent, carry_got.at[0], twin).wait_send()

    @pl.when(ring < last_fore)
    def _():
        remote(fore_out, fore_in, fore_sent, ring_got.at[0], ahead).wait_send()

    @pl.when((ring >= MID) & (ring < RING - 1))
    def _():
        remote(local_out, local_in, local_sent, ring_got.at[0], ahead).wait_send()

    @pl.when((ring < MID) | (ring == RING - 1))
    def _():
        remote(rear_out, rear_in, rear_sent, ring_got.at[0], behind).wait_send()


def shards(query_rows, key_rows, value_rows, seg_starts, norm_gain):
    _, tok, width = query_rows.shape
    dma = pltpu.SemaphoreType.DMA
    hbm = pl.BlockSpec(memory_space=pltpu.HBM)
    block = pltpu.VMEM((tok, width), key_rows.dtype)
    states = lambda heads: pltpu.VMEM((heads * HD, HD), F32)
    one = dma(())
    stay = lambda x: pltpu.with_memory_space_constraint(x, pltpu.HBM)
    out = pl.pallas_call(
        kernel,
        out_shape=jax.ShapeDtypeStruct((tok, width), query_rows.dtype),
        in_specs=[hbm] * 5,
        out_specs=pl.BlockSpec(memory_space=pltpu.VMEM),
        scratch_shapes=[
            pltpu.SMEM((1, 4), jnp.int32), block, block, block, pltpu.VMEM((1, width), F32),
            states(HEADS), states(2 * OWN),
            states(OWN), states(OWN), states(OWN), states(OWN),
            states(OWN), states(OWN), states(OWN), states(OWN), states(OWN), states(OWN),
            states(OWN), states(OWN), states(2 * OWN), states(2 * OWN),
            pltpu.VMEM((2 * OWN * HD, HD), jnp.bfloat16),
            pltpu.VMEM((tok, width), F32), pltpu.VMEM((tok, HD), F32),
            dma((11,)),
            one, dma((OWN + 1,)), one, dma((CHUNKS,)), one, dma((2 * CHUNKS,)),
            one, one, one, dma((CHUNKS,)), one, dma((2 * OWN,)),
        ],
        compiler_params=pltpu.CompilerParams(
            collective_id=0, has_side_effects=True, vmem_limit_bytes=32 * 1024 * 1024),
    )(stay(seg_starts), stay(query_rows[0]), stay(key_rows[0]), stay(value_rows[0]),
      stay(norm_gain.reshape(1, width)))
    return out.reshape(1, tok, width)


def solution(mesh):
    placed = (
        P("sess", "ctx", None),
        P("sess", "ctx", None),
        P("sess", "ctx", None),
        P("sess", None),
        P(),
    )
    return jax.shard_map(
        shards, mesh=mesh, in_specs=placed, out_specs=P("sess", "ctx", None), check_vma=False
    )
```

time: 42.1 us -> 41.3 us (0.981)
  the two profiles are of different devices: /device:TPU:48 before, /device:TPU:49 now
where the time goes in v3:
time: 41.3 us; the launch traced here: 41.2 us
  Pallas kernels  40.4 us (98%)
  local copies, waits for them, and re-layouts  0.8 us (2%)
    pallas_call x1, Pallas kernels, shards(): pl.pallas_call(kernel, out_shape=jax.ShapeDtypeStruct((tok, width), query...  40.4 us

profile of v3, /device:TPU:49, one launch (start us, length us, event | category | flops | bytes accessed | tf_op | source)
XLA Modules:
  0.0 41.2 jit_solution(1763786361988275572)
XLA Ops:
  0.0 40.4 %shard_map.55 = bf16[64,4096]{1,0:T(8,128)(2,1)S(1)} custom-call(s32[1,4]{1,0:T(1,128)} %starts_hbm.1, bf16[64,4096]{1,0:T(8,128)(2,1)} %bitcast.6, bf16[64,4096]{1,0:T(8,128)(2,1)} %bitcast.7, bf16[64,4096]{1,0:T(8,128)(2,1)} %bitcast.8, f32[1,4096]{1,0:T(1,128)} %bitcast.9), custom_call_target="tpu_custom_call" | custom-call | tf_op jit(solution)/shard_map/pallas_call | solution.py:376
  40.4 0.8 %copy.7 = bf16[1,64,4096]{2,1,0:T(8,128)(2,1)} copy(bf16[1,64,4096]{2,1,0:T(8,128)(2,1)S(1)} %bitcast.5) | data formatting | bytes 1048576

commit v4 on v3

--- a/solution.py
+++ b/solution.py
@@ -16,6 +16,7 @@
 HOP = 8
 BACK = 9
 JOIN = 8
+LATE = 3
 DRAINED = 44
 MESH = pl.DeviceIdType.MESH
 F32 = jnp.float32
@@ -72,8 +73,23 @@
     fetch_keys[0].start()
     fetch_values[0].start()
     barrier = pltpu.get_barrier_semaphore()
-    for other in (twin, across, ahead, behind):
+
+    def greet(other):
         pl.semaphore_signal(barrier, inc=1, device_id=other, device_id_type=MESH)
+
+    def rear_lands(place):
+        return (place == 1) | (place == 2) | (place >= RING - 2)
+
+    greet(twin)
+    greet(across)
+
+    @pl.when(ring > 0)
+    def _():
+        greet(behind)
+
+    @pl.when(rear_lands(ring))
+    def _():
+        greet(ahead)
 
     for n in range(1, 4):
         fetch_keys[n].start()
@@ -176,7 +192,8 @@
             own[head_rows(first + j)] = states[j]
 
     summaries(0)
-    pl.semaphore_wait(barrier, 4)
+    greeted = jnp.where(ring < RING - 1, 1, 0) + jnp.where(rear_lands((ring + RING - 1) % RING), 1, 0)
+    pl.semaphore_wait(barrier, 2 + greeted)
     for j in range(OWN):
         send_core(j).start()
     summaries(1)
@@ -246,8 +263,9 @@
         spread(half, i, p_in * arrived + p_scan * prefix)
 
     lag_local = HOP * (ring - MID)
-    lag_fore = HOP * ring
-    lag_rear = HOP * ((RING + MID - 1 - ring) % RING)
+    late = jnp.where(lax.axis_index("sess") == 0, LATE, 0)
+    lag_fore = HOP * ring + jnp.where(ring == 0, 0, late)
+    lag_rear = HOP * ((RING + MID - 1 - ring) % RING) - jnp.where(ring == 0, late, 0)
     ends = (ring > MID) & (ring < RING - 1)
     lag_prefix = jnp.where(ring <= last_fore, lag_fore, lag_rear)
     lag_back = jnp.where(ends, lag_prefix + BACK, jnp.maximum(lag_prefix + 2 * BACK, DRAINED))

time: 41.3 us -> 40.9 us (level)
  the two profiles are of different devices: /device:TPU:49 before, /device:TPU:41 now
where the time goes in v4:
time: 40.9 us; the launch traced here: 40.7 us
  Pallas kernels  39.9 us (98%)
  local copies, waits for them, and re-layouts  0.8 us (2%)
    pallas_call x1, Pallas kernels, shards(): pl.pallas_call(kernel, out_shape=jax.ShapeDtypeStruct((tok, width), query...  39.9 us

profile of v4, /device:TPU:41, one launch (start us, length us, event | category | flops | bytes accessed | tf_op | source)
XLA Modules:
  0.0 40.7 jit_solution(18078314060257711479)
XLA Ops:
  0.0 39.9 %shard_map.55 = bf16[64,4096]{1,0:T(8,128)(2,1)S(1)} custom-call(s32[1,4]{1,0:T(1,128)} %starts_hbm.1, bf16[64,4096]{1,0:T(8,128)(2,1)} %bitcast.6, bf16[64,4096]{1,0:T(8,128)(2,1)} %bitcast.7, bf16[64,4096]{1,0:T(8,128)(2,1)} %bitcast.8, f32[1,4096]{1,0:T(1,128)} %bitcast.9), custom_call_target="tpu_custom_call" | custom-call | tf_op jit(solution)/shard_map/pallas_call | solution.py:394
  39.9 0.8 %copy.7 = bf16[1,64,4096]{2,1,0:T(8,128)(2,1)} copy(bf16[1,64,4096]{2,1,0:T(8,128)(2,1)S(1)} %bitcast.5) | data formatting | bytes 1048576

commit v5 on v0

v5 whole, which is shorter than its diff:
```python
import jax
import jax.numpy as jnp
from jax import lax
from jax.experimental import pallas as pl
from jax.experimental.pallas import tpu as pltpu
from jax.sharding import PartitionSpec as P

HEADS = 32
HD = 128
OWN = 8
SUB = 4
ROWS = HD // SUB
CHUNKS = OWN * SUB
RING = 8
MID = RING // 2
HOP = 8
BACK = 9
JOIN = 8
LATE = 3
DRAINED = 44
MESH = pl.DeviceIdType.MESH
F32 = jnp.float32


def rows_at(i):
    return pl.ds(pl.multiple_of(i * ROWS, ROWS), ROWS)


def head_rows(n):
    return pl.ds(pl.multiple_of(n * HD, HD), HD)


def head_cols(h):
    return pl.ds(pl.multiple_of(h * HD, HD), HD)


def kernel(starts_hbm, q_hbm, k_hbm, v_hbm, gain_hbm, out_ref,
           starts, q_ref, k_ref, v_ref, gain_ref,
           own, core_in, chip_far, chip_own, chip_in, total,
           fore_out, fore_in, local_out, local_in, rear_out, rear_in,
           back_out, back_in, core_out, carry_in, carry, mixed, squares,
           loads, core_sent, chip_sent, fore_sent,
           local_sent, rear_sent, back_sent, back_got, carry_sent, carry_got):
    me = lax.axis_index("ctx")
    core = me % 2
    half = (me // 2) % 2
    ring = me // 4
    tok = q_ref.shape[0]
    base = me * tok

    twin = {"ctx": me + 1 - 2 * core}
    across = {"ctx": me + 2 - 4 * half}
    ahead = {"ctx": (me + 4) % (4 * RING)}
    behind = {"ctx": (me + 4 * RING - 4) % (4 * RING)}

    last_fore = MID + 1

    def group(c, z):
        return (2 * c + z) * OWN

    def group_rows(c, z):
        return pl.ds(pl.multiple_of(group(c, z) * HD, HD), OWN * HD)

    order = [(1 - core, 1 - half), (core, 1 - half), (1 - core, half), (core, half)]
    fetch_starts = pltpu.make_async_copy(starts_hbm, starts, loads.at[0])
    fetch_keys = [pltpu.make_async_copy(
        k_hbm.at[:, group_rows(*g)], k_ref.at[:, group_rows(*g)], loads.at[1 + n]) for n, g in enumerate(order)]
    fetch_values = [pltpu.make_async_copy(
        v_hbm.at[:, group_rows(*g)], v_ref.at[:, group_rows(*g)], loads.at[5 + n]) for n, g in enumerate(order)]
    fetch_rest = [pltpu.make_async_copy(q_hbm, q_ref, loads.at[9]),
                  pltpu.make_async_copy(gain_hbm, gain_ref, loads.at[10])]
    def remote(src, dst, sent, got, device):
        return pltpu.make_async_remote_copy(
            src_ref=src, dst_ref=dst, send_sem=sent, recv_sem=got,
            device_id=device, device_id_type=MESH)

    def phase(first, core_got=None, chip_got=None, ring_got=None):
        if first:
            fetch_starts.start()
            fetch_keys[0].start()
            fetch_values[0].start()
            barrier = pltpu.get_barrier_semaphore()

            def greet(other):
                pl.semaphore_signal(barrier, inc=1, device_id=other, device_id_type=MESH)

            def rear_lands(place):
                return (place == 1) | (place == 2) | (place >= RING - 2)

            greet(twin)
            greet(across)

            @pl.when(ring > 0)
            def _():
                greet(behind)

            @pl.when(rear_lands(ring))
            def _():
                greet(ahead)

            for n in range(1, 4):
                fetch_keys[n].start()
                fetch_values[n].start()
            for fetch in fetch_rest:
                fetch.start()
            fetch_starts.wait()

        start = [starts[0, n] for n in range(4)]

        def keep(low, size):
            inside = [jnp.where((s >= low) & (s < low + size), 1, 0) for s in start]
            return jnp.where(sum(inside) == 0, 1.0, 0.0).astype(F32)

        chip_base = (me // 2) * (2 * tok)
        span = 4 * tok
        ring_base = ring * span
        keep_core0 = keep(chip_base, tok)
        keep_core1 = keep(chip_base + tok, tok)
        keep_chip0 = keep(ring_base, 2 * tok)
        keep_chip1 = keep(ring_base + 2 * tok, 2 * tok)
        keep_ring = keep(ring_base, span)
        keep_local = keep(MID * span, ring_base - MID * span)
        one, nil = jnp.float32(1.0), jnp.float32(0.0)
        keep_rear = jnp.where(ring >= MID, nil, keep(ring_base + span, (MID - 1 - ring) * span))
        first_core, first_half = core == 0, half == 0
        a_own = jnp.where(first_core, keep_core1, one)
        a_in = jnp.where(first_core, one, keep_core1)
        b_own = jnp.where(first_half, keep_chip1, one)
        b_in = jnp.where(first_half, one, keep_chip1)
        e_own, e_scan = jnp.where(first_half, one, nil), jnp.where(first_half, keep_chip0, one)
        p_in, p_scan = jnp.where(first_half, nil, one), jnp.where(first_half, one, keep_chip0)
        f_own, f_pre = jnp.where(first_core, one, nil), jnp.where(first_core, keep_core0, one)
        g_in, g_pre = jnp.where(first_core, nil, one), jnp.where(first_core, one, keep_core0)

        def segment(pos):
            return sum((s <= pos).astype(jnp.int32) for s in start)

        row = lax.broadcasted_iota(jnp.int32, (tok, 1), 0) + base
        col = lax.broadcasted_iota(jnp.int32, (1, tok), 1) + base
        seg_row, seg_col = segment(row), segment(col)
        prior = sum(jnp.where(s < base, 1, 0) for s in start)
        last = sum(jnp.where(s < base + tok, 1, 0) for s in start)
        use = jnp.where(seg_row == prior, 1.0, 0.0).astype(F32)
        allowed = (row >= col) & (seg_row == seg_col)
        keep_rows = jnp.where(seg_row == last, 1.0, 0.0).astype(k_ref.dtype)

        def send_core(j):
            z = 1 - half
            return remote(own.at[head_rows(group(1 - core, z) + j)], core_in.at[head_rows(z * OWN + j)],
                          core_sent, core_got.at[j], twin)

        def send_rest():
            return remote(own.at[group_rows(1 - core, half)], core_in.at[pl.ds(half * OWN * HD, OWN * HD)],
                          core_sent, core_got.at[OWN], twin)

        def send_chip(i):
            return remote(chip_far.at[rows_at(i)], chip_in.at[rows_at(i)],
                          chip_sent, chip_got.at[i], across)

        def send_fore(i):
            return remote(fore_out.at[rows_at(i)], fore_in.at[rows_at(i)],
                          fore_sent, ring_got.at[i], ahead)

        def local_lane(place):
            return jnp.where(place == last_fore, CHUNKS, 0)

        def send_local(i, place):
            return remote(local_out.at[rows_at(i)], local_in.at[rows_at(i)],
                          local_sent, ring_got.at[local_lane(place) + i], ahead)

        def send_rear(i):
            return remote(rear_out.at[rows_at(i)], rear_in.at[rows_at(i)],
                          rear_sent, ring_got.at[CHUNKS + i], behind)

        def send_back(i):
            return remote(back_out.at[rows_at(i)], back_in.at[rows_at(i)],
                          back_sent, back_got.at[i], across)

        def send_carry(n):
            return remote(core_out.at[head_rows(n)], carry_in.at[head_rows(n)],
                          carry_sent, carry_got.at[n], twin)

        def summaries(n):
            fetch_keys[n].wait()
            fetch_values[n].wait()
            first = group(*order[n])
            states = []
            for j in range(OWN):
                cols = head_cols(first + j)
                states.append(lax.dot_general(
                    k_ref[:, cols] * keep_rows, v_ref[:, cols],
                    (((0,), (0,)), ((), ())), preferred_element_type=F32))
            for j in range(OWN):
                own[head_rows(first + j)] = states[j]

        if first:
            summaries(0)
            greeted = jnp.where(ring < RING - 1, 1, 0) + jnp.where(rear_lands((ring + RING - 1) % RING), 1, 0)
            pl.semaphore_wait(barrier, 2 + greeted)
            for j in range(OWN):
                send_core(j).start()
            summaries(1)

        def chip_total(z, j):
            return a_own * own[head_rows(group(core, z) + j)] + a_in * core_in[head_rows(z * OWN + j)]

        def far(j, _):
            send_core(j).wait_recv()
            chip_far[head_rows(j)] = chip_total(1 - half, j)
            for s in range(SUB):
                send_chip(j * SUB + s).start()
            return 0

        def near(j, _):
            chip_own[head_rows(j)] = chip_total(half, j)
            return 0

        if first:
            lax.fori_loop(0, OWN, far, 0)
            summaries(2)
            send_rest().start()
            summaries(3)

            @pl.when(ring == 0)
            def _():
                fore_in[...] = jnp.zeros_like(fore_in)

            @pl.when(ring == MID)
            def _():
                local_in[...] = jnp.zeros_like(local_in)

            @pl.when(ring == MID - 1)
            def _():
                rear_in[...] = jnp.zeros_like(rear_in)

        def intra(n, _):
            cols = [head_cols(n * 8 + m) for m in range(8)]
            scores = [lax.dot_general(
                q_ref[:, c], k_ref[:, c], (((1,), (1,)), ((), ())), preferred_element_type=F32)
                for c in cols]
            weights = [jnp.where(allowed, s, 0.0).astype(v_ref.dtype) for s in scores]
            values = [jnp.dot(w, v_ref[:, c], preferred_element_type=F32) for w, c in zip(weights, cols)]
            for c, value in zip(cols, values):
                mixed[:, c] = value
            return 0

        if first:
            for fetch in fetch_rest:
                fetch.wait()
            squares[...] = jnp.zeros_like(squares)
            lax.fori_loop(0, HEADS // 8, intra, 0)
            send_rest().wait_recv()
            lax.fori_loop(0, OWN, near, 0)

        def spread(z, i, prefix):
            n = z * CHUNKS + i
            core_out[rows_at(n)] = f_own * own[rows_at(group(core, z) * SUB + i)] + f_pre * prefix
            carry[rows_at(n)] = (g_in * core_in[rows_at(n)] + g_pre * prefix).astype(carry.dtype)

            @pl.when(i % SUB == SUB - 1)
            def _():
                send_carry(z * OWN + i // SUB).start()

        def finish(i, prefix):
            arrived, mine = chip_in[rows_at(i)], chip_own[rows_at(i)]
            back_out[rows_at(i)] = e_own * mine + e_scan * prefix
            send_back(i).start()
            spread(half, i, p_in * arrived + p_scan * prefix)

        lag_local = HOP * (ring - MID)
        late = jnp.where(lax.axis_index("sess") == 0, LATE, 0)
        lag_fore = HOP * ring + jnp.where(ring == 0, 0, late)
        lag_rear = HOP * ((RING + MID - 1 - ring) % RING) - jnp.where(ring == 0, late, 0)
        ends = (ring > MID) & (ring < RING - 1)
        lag_prefix = jnp.where(ring <= last_fore, lag_fore, lag_rear)
        lag_back = jnp.where(ends, lag_prefix + BACK, jnp.maximum(lag_prefix + 2 * BACK, DRAINED))
        lag_join = lag_back + SUB + JOIN

        def settle(j):
            heads, states = [], []
            for z in (half, 1 - half):
                heads.append(group(core, z) + j)
                states.append(carry[head_rows(z * OWN + j)])
            for z in (half, 1 - half):
                send_carry(z * OWN + j).wait_recv()
                heads.append(group(1 - core, z) + j)
                states.append(carry_in[head_rows(z * OWN + j)].astype(carry.dtype))
            cols = [head_cols(h) for h in heads]
            inter = [jnp.dot(q_ref[:, c], state, preferred_element_type=F32) for c, state in zip(cols, states)]
            values = [mixed[:, c] + use * part for c, part in zip(cols, inter)]
            for c, value in zip(cols, values):
                mixed[:, c] = value
            squares[...] += sum(value * value for value in values)

        def active(s, lag):
            return (s >= lag) & (s < lag + CHUNKS)

        def step(s, _):
            if first:
                @pl.when(s < CHUNKS)
                def _():
                    send_chip(s).wait_recv()
                    total[rows_at(s)] = b_own * chip_own[rows_at(s)] + b_in * chip_in[rows_at(s)]

                @pl.when((ring >= MID) & active(s, lag_local))
                def _():
                    i = s - lag_local

                    @pl.when(ring > MID)
                    def _():
                        send_local(i, ring).wait_recv()

                    @pl.when(ring < RING - 1)
                    def _():
                        local_out[rows_at(i)] = total[rows_at(i)] + keep_ring * local_in[rows_at(i)]
                        send_local(i, ring + 1).start()

                @pl.when((ring <= last_fore) & active(s, lag_fore))
                def _():
                    i = s - lag_fore

                    @pl.when(ring > 0)
                    def _():
                        send_fore(i).wait_recv()

                    prefix = fore_in[rows_at(i)]

                    @pl.when(ring < last_fore)
                    def _():
                        fore_out[rows_at(i)] = total[rows_at(i)] + keep_ring * prefix
                        send_fore(i).start()

                    finish(i, prefix)

                @pl.when(((ring < MID) | (ring > last_fore)) & active(s, lag_rear))
                def _():
                    i = s - lag_rear

                    @pl.when(ring != MID - 1)
                    def _():
                        send_rear(i).wait_recv()

                    @pl.when((ring < MID) | (ring == RING - 1))
                    def _():
                        rear_out[rows_at(i)] = rear_in[rows_at(i)] + keep_rear * total[rows_at(i)]
                        send_rear(i).start()

                    @pl.when(ring > last_fore)
                    def _():
                        finish(i, local_in[rows_at(i)] + keep_local * rear_in[rows_at(i)])

            @pl.when(active(s, lag_back))
            def _():
                i = s - lag_back
                send_back(i).wait_recv()
                spread(1 - half, i, back_in[rows_at(i)])

            @pl.when((s >= lag_join) & ((s - lag_join) % SUB == 0))
            def _():
                settle((s - lag_join) // SUB)

            return 0

        streamed = CHUNKS + jnp.maximum(
            jnp.where(ring <= last_fore, lag_fore, 0),
            jnp.where((ring < MID) | (ring > last_fore), lag_rear, 0))
        if first:
            lax.fori_loop(0, streamed, step, 0)
        else:
            lax.fori_loop(streamed, lag_join + CHUNKS - SUB + 1, step, 0)

    pl.run_scoped(
        lambda *got: phase(True, *got),
        pltpu.SemaphoreType.DMA((OWN + 1,)), pltpu.SemaphoreType.DMA((CHUNKS,)), pltpu.SemaphoreType.DMA((2 * CHUNKS,)))
    phase(False)
    mean = jnp.sum(squares[...], axis=-1, keepdims=True) * (1.0 / (HEADS * HD))
    scale = lax.rsqrt(mean + 1e-05)
    for h in range(HEADS):
        cols = slice(h * HD, (h + 1) * HD)
        out_ref[:, cols] = (mixed[:, cols] * scale * gain_ref[:, cols]).astype(out_ref.dtype)

    for z in range(2):
        remote(own.at[group_rows(1 - core, z)], core_in.at[pl.ds(z * OWN * HD, OWN * HD)],
               core_sent, back_got.at[0], twin).wait_send()
    remote(chip_far, chip_in, chip_sent, back_got.at[0], across).wait_send()
    remote(back_out, back_in, back_sent, back_got.at[0], across).wait_send()
    remote(core_out, carry_in, carry_sent, carry_got.at[0], twin).wait_send()

    @pl.when(ring < last_fore)
    def _():
        remote(fore_out, fore_in, fore_sent, back_got.at[0], ahead).wait_send()

    @pl.when((ring >= MID) & (ring < RING - 1))
    def _():
        remote(local_out, local_in, local_sent, back_got.at[0], ahead).wait_send()

    @pl.when((ring < MID) | (ring == RING - 1))
    def _():
        remote(rear_out, rear_in, rear_sent, back_got.at[0], behind).wait_send()


def shards(query_rows, key_rows, value_rows, seg_starts, norm_gain):
    _, tok, width = query_rows.shape
    dma = pltpu.SemaphoreType.DMA
    hbm = pl.BlockSpec(memory_space=pltpu.HBM)
    block = pltpu.VMEM((tok, width), key_rows.dtype)
    states = lambda heads: pltpu.VMEM((heads * HD, HD), F32)
    one = dma(())
    stay = lambda x: pltpu.with_memory_space_constraint(x, pltpu.HBM)
    out = pl.pallas_call(
        kernel,
        out_shape=jax.ShapeDtypeStruct((tok, width), query_rows.dtype),
        in_specs=[hbm] * 5,
        out_specs=pl.BlockSpec(memory_space=pltpu.VMEM),
        scratch_shapes=[
            pltpu.SMEM((1, 4), jnp.int32), block, block, block, pltpu.VMEM((1, width), F32),
            states(HEADS), states(2 * OWN),
            states(OWN), states(OWN), states(OWN), states(OWN),
            states(OWN), states(OWN), states(OWN), states(OWN), states(OWN), states(OWN),
            states(OWN), states(OWN), states(2 * OWN), states(2 * OWN),
            pltpu.VMEM((2 * OWN * HD, HD), jnp.bfloat16),
            pltpu.VMEM((tok, width), F32), pltpu.VMEM((tok, HD), F32),
            dma((11,)),
            one, one, one, one, one, one, dma((CHUNKS,)), one, dma((2 * OWN,)),
        ],
        compiler_params=pltpu.CompilerParams(
            collective_id=0, has_side_effects=True, vmem_limit_bytes=32 * 1024 * 1024),
    )(stay(seg_starts), stay(query_rows[0]), stay(key_rows[0]), stay(value_rows[0]),
      stay(norm_gain.reshape(1, width)))
    return out.reshape(1, tok, width)


def solution(mesh):
    placed = (
        P("sess", "ctx", None),
        P("sess", "ctx", None),
        P("sess", "ctx", None),
        P("sess", None),
        P(),
    )
    return jax.shard_map(
        shards, mesh=mesh, in_specs=placed, out_specs=P("sess", "ctx", None), check_vma=False
    )
```

time: 535 us -> 39.9 us (0.07)
  the two profiles are of different devices: /device:TPU:1 before, /device:TPU:41 now
where the time goes in v5:
time: 39.9 us; the launch traced here: 39.8 us
  Pallas kernels  39 us (98%)
  local copies, waits for them, and re-layouts  0.8 us (2%)
    pallas_call x1, Pallas kernels, shards(): pl.pallas_call(kernel, out_shape=jax.ShapeDtypeStruct((tok, width), query...  39 us

profile of v5, /device:TPU:41, one launch (start us, length us, event | category | flops | bytes accessed | tf_op | source)
XLA Modules:
  0.0 39.8 jit_solution(8375269808730733157)
XLA Ops:
  0.0 39.0 %shard_map.55 = bf16[64,4096]{1,0:T(8,128)(2,1)S(1)} custom-call(s32[1,4]{1,0:T(1,128)} %starts_hbm.1, bf16[64,4096]{1,0:T(8,128)(2,1)} %bitcast.6, bf16[64,4096]{1,0:T(8,128)(2,1)} %bitcast.7, bf16[64,4096]{1,0:T(8,128)(2,1)} %bitcast.8, f32[1,4096]{1,0:T(1,128)} %bitcast.9), custom_call_target="tpu_custom_call" | custom-call | tf_op jit(solution)/shard_map/pallas_call | solution.py:410
  39.0 0.8 %copy.7 = bf16[1,64,4096]{2,1,0:T(8,128)(2,1)} copy(bf16[1,64,4096]{2,1,0:T(8,128)(2,1)S(1)} %bitcast.5) | data formatting | bytes 1048576

commit v6 on v5

--- a/solution.py
+++ b/solution.py
@@ -8,16 +8,16 @@
 HEADS = 32
 HD = 128
 OWN = 8
-SUB = 4
+SUB = 8
 ROWS = HD // SUB
 CHUNKS = OWN * SUB
 RING = 8
 MID = RING // 2
-HOP = 8
-BACK = 9
-JOIN = 8
-LATE = 3
-DRAINED = 44
+HOP = 16
+BACK = 17
+JOIN = 14
+LATE = 6
+DRAINED = 86
 MESH = pl.DeviceIdType.MESH
 F32 = jnp.float32
 

time: 39.9 us -> 39.9 us (level)
  no operation moved by 1% of the time
where the time goes in v6:
time: 39.9 us; the launch traced here: 39.8 us
  Pallas kernels  39 us (98%)
  local copies, waits for them, and re-layouts  0.8 us (2%)
    pallas_call x1, Pallas kernels, shards(): pl.pallas_call(kernel, out_shape=jax.ShapeDtypeStruct((tok, width), query...  39 us

profile of v6, /device:TPU:41, one launch (start us, length us, event | category | flops | bytes accessed | tf_op | source)
XLA Modules:
  0.0 39.8 jit_solution(428173865957140570)
XLA Ops:
  0.0 39.0 %shard_map.55 = bf16[64,4096]{1,0:T(8,128)(2,1)S(1)} custom-call(s32[1,4]{1,0:T(1,128)} %starts_hbm.1, bf16[64,4096]{1,0:T(8,128)(2,1)} %bitcast.6, bf16[64,4096]{1,0:T(8,128)(2,1)} %bitcast.7, bf16[64,4096]{1,0:T(8,128)(2,1)} %bitcast.8, f32[1,4096]{1,0:T(1,128)} %bitcast.9), custom_call_target="tpu_custom_call" | custom-call | tf_op jit(solution)/shard_map/pallas_call | solution.py:410
  39.0 0.8 %copy.7 = bf16[1,64,4096]{2,1,0:T(8,128)(2,1)} copy(bf16[1,64,4096]{2,1,0:T(8,128)(2,1)S(1)} %bitcast.5) | data formatting | bytes 1048576
